TPU v7x, 256 devices: a whole 4x4x8 slice. The times are simulated.
256 devices in a mesh: pipe: 16 (over y_hi, z), vocab: 16 (over y_lo, x, core).
Axes of the slice: x: 4, y: 4 (y_hi: 2, y_lo: 2; y = y_hi * 2 + y_lo), z: 8, core: 2. Of those that a mesh axis runs over, the one named last changes fastest.
Arguments:
- final_hidden: bfloat16 [512, 4608], P('pipe', 'vocab'), may hold values from -6 to 6
- tied_table: bfloat16 [163840, 4608], P(('pipe', 'vocab')), may hold values from -1.2 to 1.2
- target_ids: int32 [512], replicated, may hold values from 0 to 163839
- input_ids: int32 [512], replicated, may hold values from 0 to 163839
- embed_cot: bfloat16 [512, 4608], P('pipe', 'vocab'), may hold values from -0.3125 to 0.3125
Outputs:
- grad_table: bfloat16 [163840, 4608], P(('pipe', 'vocab'))
- grad_hidden: float32 [512, 4608], P('pipe', 'vocab')
- token_loss: float32 [512], P('pipe')
All inputs are finite; a program needn't handle non-finite values.
Results may differ from a plain program's by a relative error of at most 0.01.
Values may be sent and summed in bfloat16 or wider, within the bound.
A program may use at most 128 MiB of HBM per device.

v0:
```python
import jax
import jax.numpy as jnp
from jax import lax
from jax.sharding import PartitionSpec as P

D = 4608


def local(final_hidden, tied_table, target_ids, input_ids, embed_cot):
    whole_h, whole_c = (
        lax.all_gather(final_hidden, "vocab", axis=1, tiled=True),
        lax.all_gather(embed_cot, "vocab", axis=1, tiled=True),
    )
    whole_h, whole_c = (
        lax.all_gather(whole_h, "pipe", axis=0, tiled=True),
        lax.all_gather(whole_c, "pipe", axis=0, tiled=True),
    )
    rows_dev = tied_table.shape[0]
    offset = lax.axis_index(("pipe", "vocab")) * rows_dev
    vocab_ids = offset + jnp.arange(rows_dev, dtype=jnp.int32)
    logits = jnp.einsum("td,vd->tv", whole_h, tied_table, preferred_element_type=jnp.float32)
    tanh_part = jnp.tanh(logits / 30.0)
    capped = 30.0 * tanh_part
    exponent = jnp.exp(capped)
    target_mask = vocab_ids[None, :] == target_ids[:, None]
    local_sum = jnp.sum(exponent, axis=1)
    local_target = jnp.sum(jnp.where(target_mask, capped, 0.0), axis=1)
    sum_exp, target_logit = lax.psum((local_sum, local_target), ("pipe", "vocab"))
    token_loss = jnp.log(sum_exp) - target_logit
    dlogits = (
        (exponent / sum_exp[:, None] - target_mask.astype(jnp.float32))
        * (1.0 - tanh_part * tanh_part)
    ).astype(jnp.bfloat16)
    head_grad = jnp.einsum("tv,td->vd", dlogits, whole_h, preferred_element_type=jnp.float32)
    input_mask = (vocab_ids[:, None] == input_ids[None, :]).astype(jnp.bfloat16)
    embed_grad = jnp.dot(input_mask, whole_c, preferred_element_type=jnp.float32)
    grad_table = (head_grad + float(D) ** 0.5 * embed_grad).astype(jnp.bfloat16)
    products = jnp.dot(dlogits, tied_table, preferred_element_type=jnp.float32)
    partial_value = lax.psum_scatter(
        products.astype(jnp.bfloat16), "vocab", scatter_dimension=1, tiled=True
    ).astype(jnp.float32)
    grad_hidden = lax.psum_scatter(partial_value, "pipe", scatter_dimension=0, tiled=True)
    held = final_hidden.shape[0]
    loss_shard = lax.dynamic_slice_in_dim(token_loss, lax.axis_index("pipe") * held, held)
    return (grad_table, grad_hidden, loss_shard)


def solution(mesh):
    placed = (P("pipe", "vocab"), P(("pipe", "vocab"), None), P(), P(), P("pipe", "vocab"))
    return jax.shard_map(
        local,
        mesh=mesh,
        in_specs=placed,
        out_specs=(P(("pipe", "vocab"), None), P("pipe", "vocab"), P("pipe")),
        check_vma=False,
    )
```

profile of v0, /device:TPU:2, one launch (start us, length us, event | category | flops | bytes accessed | tf_op | source)
XLA Modules:
  0.0 609.2 jit_solution(8618035419654364876)
XLA Ops:
  7.2 0.0 copy-start
  7.2 0.0 all-gather.5.cloned.1.call-start
  7.2 19.4 %all-gather = bf16[16,288,32]{1,2,0:T(8,128)(2,1)S(1)} all-gather(bf16[1,288,32]{1,2,0:T(8,128)(2,1)} %bitcast.20), channel_id=1, replica_groups=mesh['pipe'=16,'vocab'=16] {'vocab'}, dimensions={0}, use_global_device_ids=true | all-gather | bytes 313344 | tf_op jit(solution)/shard_map/all_gather | solution.py:11
  26.7 0.1 copy.12
  26.8 1.1 reshape.18
  27.9 0.0 all-gather.5.cloned.1.call-update
  27.9 0.0 reduce-scatter.5.cloned.1.call-start
  28.0 105.3 %all-gather.5.cloned.1.call-done = bf16[512,4608]{1,0:T(8,128)(2,1)} async-done(((bf16[32,4608]{1,0:T(8,128)(2,1)}), bf16[512,4608]{1,0:T(8,128)(2,1)}) %all-gather.5.cloned.1.call-update) | async-done | bytes 4718608 | tf_op jit(solution)/shard_map/all_gather | solution.py:15
  133.3 0.0 copy-done
  133.3 7.8 %fusion.4 = (f32[512]{0:T(512)S(1)}, f32[512]{0:T(512)S(1)}, f32[512,640]{1,0:T(8,128)S(1)}) fusion(s32[640]{0:T(1024)S(1)} %iota_add_fusion, s32[512]{0:T(512)S(1)} %copy-done, bf16[512,4608]{1,0:T(8,128)(2,1)} %all-gather.5.cloned.1.call-done, bf16[640,4608]{1,0:T(8,128)(2,1)} %param.6), kind=kOutput, calls=%fused_computation.9 | convolution fusion | flops 3021863936 | bytes 11936256 | tf_op jit(solution)/shard_map/td,vd->tv/dot_general | solution.py:21
  141.0 72.8 %all-reduce = (f32[512]{0:T(512)S(1)}, f32[512]{0:T(512)S(1)}) all-reduce(f32[512]{0:T(512)S(1)} %get-tuple-element.13, f32[512]{0:T(512)S(1)} %get-tuple-element.12), channel_id=1, replica_groups=mesh['pipe'=16,'vocab'=16] {'pipe','vocab'}, use_global_device_ids=true, to_apply=%region_1.2 | all-reduce | flops 1024 | bytes 8192 | tf_op jit(solution)/shard_map/psum | solution.py:28
  213.8 9.8 %convolution_convert_fusion = bf16[512,4608]{0,1:T(8,128)(2,1)} fusion(bf16[640,4608]{1,0:T(8,128)(2,1)} %param.6, f32[512,640]{1,0:T(8,128)S(1)} %get-tuple-element.16, s32[640]{0:T(1024)S(1)} %iota_add_fusion, f32[512]{0:T(512)S(1)} %get-tuple-element.14, s32[512]{0:T(512)S(1)} %copy-done), kind=kOutput, calls=%fused_computation.1 | convolution fusion | flops 3025207296 | bytes 11934208 | tf_op jit(solution)/shard_map/dot_general | solution.py:38
  223.6 0.0 copy-start.1
  223.6 0.0 reduce-scatter.5.cloned.1.call-update
  223.6 0.0 all-gather.7.cloned.1.call-start
  223.7 0.7 copy-done.1
  224.4 19.9 %all-gather.1 = bf16[16,288,32]{1,2,0:T(8,128)(2,1)S(1)} all-gather(bf16[1,288,32]{1,2,0:T(8,128)(2,1)S(1)} %bitcast.21), channel_id=1, replica_groups=mesh['pipe'=16,'vocab'=16] {'vocab'}, dimensions={0}, use_global_device_ids=true | all-gather | bytes 313344 | tf_op jit(solution)/shard_map/all_gather | solution.py:12
  244.3 0.1 copy.13
  244.4 1.1 reshape.20
  245.5 0.0 all-gather.7.cloned.1.call-update
  245.6 0.2 reduce-scatter.7.cloned.1.call-start
  245.8 10.2 %fusion.9 = f32[640,4608]{1,0:T(8,128)} fusion(bf16[512,4608]{1,0:T(8,128)(2,1)} %all-gather.5.cloned.1.call-done, f32[512,640]{1,0:T(8,128)S(1)} %get-tuple-element.16, s32[640]{0:T(1024)S(1)} %iota_add_fusion, f32[512]{0:T(512)S(1)} %get-tuple-element.14, s32[512]{0:T(512)S(1)} %copy-done), kind=kOutput, calls=%fused_computation.16 | convolution fusion | flops 3022848000 | bytes 17832448 | tf_op jit(solution)/shard_map/tv,td->vd/dot_general | solution.py:34
  256.0 0.0 copy-start.2
  256.0 32.3 %reduce-scatter.5.cloned.1.call-done = bf16[512,288]{0,1:T(8,128)(2,1)} async-done(((bf16[512,4608]{0,1:T(8,128)(2,1)}), bf16[512,288]{0,1:T(8,128)(2,1)}) %reduce-scatter.5.cloned.1.call-update) | async-done | bytes 294928 | tf_op jit(solution)/shard_map/reduce_scatter | solution.py:39
  288.3 2.0 copy.15
  290.3 0.0 reduce-scatter.7.cloned.1.call-update
  290.3 0.6 dynamic_slice.3
  290.9 106.2 %all-gather.7.cloned.1.call-done = bf16[512,4608]{1,0:T(8,128)(2,1)} async-done(((bf16[32,4608]{1,0:T(8,128)(2,1)}), bf16[512,4608]{1,0:T(8,128)(2,1)}) %all-gather.7.cloned.1.call-update) | async-done | bytes 4718608 | tf_op jit(solution)/shard_map/all_gather | solution.py:16
  397.1 0.0 copy-done.2
  397.1 9.3 %add_convert_fusion = bf16[640,4608]{1,0:T(8,128)(2,1)} fusion(f32[640,4608]{1,0:T(8,128)} %fusion.9, bf16[512,4608]{1,0:T(8,128)(2,1)} %all-gather.7.cloned.1.call-done, s32[512]{0:T(512)S(1)} %copy-done.2, s32[640]{0:T(1024)S(1)} %iota_add_fusion), kind=kOutput, calls=%fused_computation | convolution fusion | flops 3029073920 | bytes 22417920 | tf_op jit(solution)/shard_map/dot_general | solution.py:36
  406.3 196.3 %reduce-scatter.7.cloned.1.call-done = f32[32,288]{1,0:T(8,128)} async-done(((f32[512,288]{1,0:T(8,128)}), f32[32,288]{1,0:T(8,128)}) %reduce-scatter.7.cloned.1.call-update) | async-done | bytes 36880
  (2 shorter events, 0.0 us)
Async XLA Ops:
  7.2 126.1 %copy-start = (s32[512]{0:T(512)S(1)}, s32[512]{0:T(512)}, u32[]{:S(2)}) copy-start(s32[512]{0:T(512)} %param.7) | copy-start | bytes 6148
  7.2 126.1 %all-gather.5.cloned.1.call-start = ((), (), s32[]{:S(2)}) async-start(), calls=%async_computation.2 | async-start | bytes 5013504 | tf_op jit(solution)/shard_map/all_gather | solution.py:15
  27.9 260.3 %reduce-scatter.5.cloned.1.call-start = ((), (), s32[]{:S(2)}) async-start(), calls=%async_computation.4 | async-start | bytes 5013504 | tf_op jit(solution)/shard_map/reduce_scatter | solution.py:39
  223.6 0.7 copy-start.1
  223.6 173.4 %all-gather.7.cloned.1.call-start = ((), (), s32[]{:S(2)}) async-start(), calls=%async_computation.3 | async-start | bytes 5013504 | tf_op jit(solution)/shard_map/all_gather | solution.py:16
  245.6 357.1 %reduce-scatter.7.cloned.1.call-start = ((), (), s32[]{:S(2)}) async-start(), calls=%async_computation.5 | async-start | bytes 835584
  256.0 141.1 %copy-start.2 = (s32[512]{0:T(512)S(1)}, s32[512]{0:T(512)}, u32[]{:S(2)}) copy-start(s32[512]{0:T(512)} %param.8) | copy-start | bytes 6148
Sparse Core Ops, SparseCore 0:
  28.0 105.1 all-gather.4
  223.8 64.4 reduce-scatter.4
  290.9 106.1 all-gather.6
  401.3 201.2 reduce-scatter.6
where the time goes:
time: 610 us; the launch traced here: 609 us
  waiting for transfers between devices  440 us (72%)
  blocking collectives  112 us (18%)
  matrix products  37 us (6%)
  between operations  13.8 us (2%)
    unnamed x5, waiting for transfers between devices  196 us
    all_gather x1, waiting for transfers between devices, local(): lax.all_gather(whole_c, 'pipe', axis=0, tiled=True)  106 us
    all_gather x1, waiting for transfers between devices, local(): lax.all_gather(whole_h, 'pipe', axis=0, tiled=True)  105 us
    psum x1, blocking collectives, local(): lax.psum((local_sum, local_target), ('pipe', 'vocab'))  72.8 us
    reduce_scatter x1, waiting for transfers between devices, local(): lax.psum_scatter(products.astype(jnp.bfloat16), 'vocab', scatter_dimensio...  32.3 us
    all_gather x1, blocking collectives, local(): lax.all_gather(embed_cot, 'vocab', axis=1, tiled=True)  19.9 us
    all_gather x1, blocking collectives, local(): lax.all_gather(final_hidden, 'vocab', axis=1, tiled=True)  19.4 us
  transfers between devices with their start and end apart: 4, of which 4 were waited for; matrix products, arithmetic and copies ran while one was open for 4% of the time, Pallas kernels for 0%

commit v1 on v0

--- a/solution.py
+++ b/solution.py
@@ -6,15 +6,24 @@
 D = 4608
 
 
+def watch_sectors(message):
+    return jnp.concatenate(
+        lax.all_to_all(
+            jnp.stack([message for _ in range(lax.axis_size("pipe"))]),
+            axis_name="pipe",
+            split_axis=0,
+            concat_axis=0,
+        ),
+        axis=0,
+    )
+
+
 def local(final_hidden, tied_table, target_ids, input_ids, embed_cot):
     whole_h, whole_c = (
         lax.all_gather(final_hidden, "vocab", axis=1, tiled=True),
         lax.all_gather(embed_cot, "vocab", axis=1, tiled=True),
     )
-    whole_h, whole_c = (
-        lax.all_gather(whole_h, "pipe", axis=0, tiled=True),
-        lax.all_gather(whole_c, "pipe", axis=0, tiled=True),
-    )
+    whole_h, whole_c = (lax.all_gather(whole_h, "pipe", axis=0, tiled=True), watch_sectors(whole_c))
     rows_dev = tied_table.shape[0]
     offset = lax.axis_index(("pipe", "vocab")) * rows_dev
     vocab_ids = offset + jnp.arange(rows_dev, dtype=jnp.int32)

time: 610 us -> 545 us (0.89)
  waiting for transfers between devices: 440 us -> 368 us
    all_gather x1 -> x0, waiting for transfers between devices: 106 us -> none  [local(): lax.all_gather(whole_c, 'pipe', axis=0, tiled=True)]
    all_to_all x0 -> x1, waiting for transfers between devices: none -> 65.5 us  [watch_sectors(): lax.all_to_all(jnp.stack([message for _ in range(lax.axis_size('pipe'))])...]
    unnamed x5 -> x4, waiting for transfers between devices: 196 us -> 166 us
  transfers between devices with their start and end apart: 4 -> 4, of which waited for: 4 -> 4; matrix products, arithmetic and copies ran while one was open for 4% -> 5% of each run, Pallas kernels for 0% -> 0%
where the time goes in v1:
time: 545 us; the launch traced here: 544 us
  waiting for transfers between devices  368 us (68%)
  blocking collectives  112 us (21%)
  matrix products  37.1 us (7%)
  between operations  13.8 us (3%)
  local copies, waits for them, and re-layouts  7.71 us (1%)
    unnamed x4, waiting for transfers between devices  166 us
    all_gather x1, waiting for transfers between devices, local(): lax.all_gather(whole_h, 'pipe', axis=0, tiled=True)  105 us
    psum x1, blocking collectives, local(): lax.psum((local_sum, local_target), ('pipe', 'vocab'))  72.8 us
    all_to_all x1, waiting for transfers between devices, watch_sectors(): lax.all_to_all(jnp.stack([message for _ in range(lax.axis_size('pipe'))])...  65.5 us
    reduce_scatter x1, waiting for transfers between devices, local(): lax.psum_scatter(products.astype(jnp.bfloat16), 'vocab', scatter_dimensio...  31.1 us
    all_gather x1, blocking collectives, local(): lax.all_gather(embed_cot, 'vocab', axis=1, tiled=True)  20 us
    all_gather x1, blocking collectives, local(): lax.all_gather(final_hidden, 'vocab', axis=1, tiled=True)  19.4 us
  transfers between devices with their start and end apart: 4, of which 4 were waited for; matrix products, arithmetic and copies ran while one was open for 5% of the time, Pallas kernels for 0%

profile of v1, /device:TPU:2, one launch (start us, length us, event | category | flops | bytes accessed | tf_op | source)
XLA Modules:
  0.0 544.3 jit_solution(8950974292373036436)
XLA Ops:
  7.2 0.0 copy-start
  7.2 0.0 all-gather.4.cloned.1.call-start
  7.2 19.4 %all-gather = bf16[16,288,32]{1,2,0:T(8,128)(2,1)S(1)} all-gather(bf16[1,288,32]{1,2,0:T(8,128)(2,1)} %bitcast.21), channel_id=1, replica_groups=mesh['pipe'=16,'vocab'=16] {'vocab'}, dimensions={0}, use_global_device_ids=true | all-gather | bytes 313344 | tf_op jit(solution)/shard_map/all_gather | solution.py:23
  26.7 0.1 copy.13
  26.8 1.1 reshape.24
  27.9 0.0 all-gather.4.cloned.1.call-update
  27.9 0.0 reduce-scatter.5.cloned.1.call-start
  28.0 105.3 %all-gather.4.cloned.1.call-done = bf16[512,4608]{1,0:T(8,128)(2,1)} async-done(((bf16[32,4608]{1,0:T(8,128)(2,1)}), bf16[512,4608]{1,0:T(8,128)(2,1)}) %all-gather.4.cloned.1.call-update) | async-done | bytes 4718608 | tf_op jit(solution)/shard_map/all_gather | solution.py:26
  133.3 0.0 copy-done
  133.3 7.8 %fusion.4 = (f32[512]{0:T(512)S(1)}, f32[512]{0:T(512)S(1)}, f32[512,640]{1,0:T(8,128)S(1)}) fusion(s32[640]{0:T(1024)S(1)} %iota_add_fusion, s32[512]{0:T(512)S(1)} %copy-done, bf16[512,4608]{1,0:T(8,128)(2,1)} %all-gather.4.cloned.1.call-done, bf16[640,4608]{1,0:T(8,128)(2,1)} %param.6), kind=kOutput, calls=%fused_computation.9 | convolution fusion | flops 3021863936 | bytes 11936256 | tf_op jit(solution)/shard_map/td,vd->tv/dot_general | solution.py:30
  141.0 72.8 %all-reduce = (f32[512]{0:T(512)S(1)}, f32[512]{0:T(512)S(1)}) all-reduce(f32[512]{0:T(512)S(1)} %get-tuple-element.13, f32[512]{0:T(512)S(1)} %get-tuple-element.12), channel_id=1, replica_groups=mesh['pipe'=16,'vocab'=16] {'pipe','vocab'}, use_global_device_ids=true, to_apply=%region_1.2 | all-reduce | flops 1024 | bytes 8192 | tf_op jit(solution)/shard_map/psum | solution.py:37
  213.9 9.9 %convolution_convert_fusion = bf16[512,4608]{0,1:T(8,128)(2,1)} fusion(bf16[640,4608]{1,0:T(8,128)(2,1)} %param.6, f32[512,640]{1,0:T(8,128)S(1)} %get-tuple-element.16, s32[640]{0:T(1024)S(1)} %iota_add_fusion, f32[512]{0:T(512)S(1)} %get-tuple-element.14, s32[512]{0:T(512)S(1)} %copy-done), kind=kOutput, calls=%fused_computation.1 | convolution fusion | flops 3025207296 | bytes 11934208 | tf_op jit(solution)/shard_map/dot_general | solution.py:47
  223.8 0.0 copy-start.1
  223.8 0.0 reduce-scatter.5.cloned.1.call-update
  223.8 0.7 copy-done.1
  224.5 20.0 %all-gather.1 = bf16[16,288,32]{1,2,0:T(8,128)(2,1)S(1)} all-gather(bf16[1,288,32]{1,2,0:T(8,128)(2,1)S(1)} %bitcast.22), channel_id=1, replica_groups=mesh['pipe'=16,'vocab'=16] {'vocab'}, dimensions={0}, use_global_device_ids=true | all-gather | bytes 313344 | tf_op jit(solution)/shard_map/all_gather | solution.py:24
  244.5 0.1 copy.14
  244.6 0.4 reshape.26
  245.0 2.6 stack.2
  247.6 4.9 all-to-all-start
  252.6 0.2 reduce-scatter.7.cloned.1.call-start
  252.8 10.2 %fusion.9 = f32[640,4608]{1,0:T(8,128)} fusion(bf16[512,4608]{1,0:T(8,128)(2,1)} %all-gather.4.cloned.1.call-done, f32[512,640]{1,0:T(8,128)S(1)} %get-tuple-element.16, s32[640]{0:T(1024)S(1)} %iota_add_fusion, f32[512]{0:T(512)S(1)} %get-tuple-element.14, s32[512]{0:T(512)S(1)} %copy-done), kind=kOutput, calls=%fused_computation.16 | convolution fusion | flops 3022848000 | bytes 17832448 | tf_op jit(solution)/shard_map/tv,td->vd/dot_general | solution.py:43
  263.0 0.0 copy-start.2
  263.0 31.1 %reduce-scatter.5.cloned.1.call-done = bf16[512,288]{0,1:T(8,128)(2,1)} async-done(((bf16[512,4608]{0,1:T(8,128)(2,1)}), bf16[512,288]{0,1:T(8,128)(2,1)}) %reduce-scatter.5.cloned.1.call-update) | async-done | bytes 294928 | tf_op jit(solution)/shard_map/reduce_scatter | solution.py:48
  294.1 2.0 copy.16
  296.1 0.0 reduce-scatter.7.cloned.1.call-update
  296.2 0.6 dynamic_slice.3
  296.8 65.5 %all-to-all-done = bf16[16,32,4608]{2,1,0:T(8,128)(2,1)} async-done(((bf16[16,32,4608]{2,1,0:T(8,128)(2,1)}), bf16[16,32,4608]{2,1,0:T(8,128)(2,1)}, u32[]{:S(2)}, u32[]{:S(2)}) %all-to-all-start) | async-done | bytes 4718624 | tf_op jit(solution)/shard_map/all_to_all | solution.py:11
  362.3 0.0 copy-done.2
  362.3 9.3 %add_convert_fusion = bf16[640,4608]{1,0:T(8,128)(2,1)} fusion(f32[640,4608]{1,0:T(8,128)} %fusion.9, bf16[512,4608]{1,0:T(8,128)(2,1)} %bitcast.6, s32[512]{0:T(512)S(1)} %copy-done.2, s32[640]{0:T(1024)S(1)} %iota_add_fusion), kind=kOutput, calls=%fused_computation | convolution fusion | flops 3029073920 | bytes 22417920 | tf_op jit(solution)/shard_map/dot_general | solution.py:45
  371.6 166.2 %reduce-scatter.7.cloned.1.call-done = f32[32,288]{1,0:T(8,128)} async-done(((f32[512,288]{1,0:T(8,128)}), f32[32,288]{1,0:T(8,128)}) %reduce-scatter.7.cloned.1.call-update) | async-done | bytes 36880
  (2 shorter events, 0.0 us)
Async XLA Ops:
  7.2 126.1 %copy-start = (s32[512]{0:T(512)S(1)}, s32[512]{0:T(512)}, u32[]{:S(2)}) copy-start(s32[512]{0:T(512)} %param.7) | copy-start | bytes 6148
  7.2 126.1 %all-gather.4.cloned.1.call-start = ((), (), s32[]{:S(2)}) async-start(), calls=%async_computation.3 | async-start | bytes 5013504 | tf_op jit(solution)/shard_map/all_gather | solution.py:26
  27.9 266.2 %reduce-scatter.5.cloned.1.call-start = ((), (), s32[]{:S(2)}) async-start(), calls=%async_computation.4 | async-start | bytes 5013504 | tf_op jit(solution)/shard_map/reduce_scatter | solution.py:48
  223.8 0.7 copy-start.1
  247.6 114.7 %all-to-all-start = ((bf16[16,32,4608]{2,1,0:T(8,128)(2,1)}), bf16[16,32,4608]{2,1,0:T(8,128)(2,1)}, u32[]{:S(2)}, u32[]{:S(2)}) async-start(bf16[16,32,4608]{2,1,0:T(8,128)(2,1)} %stack.2), calls=%async_computation | async-start | bytes 9437184 | tf_op jit(solution)/shard_map/all_to_all | solution.py:11
  252.6 285.2 %reduce-scatter.7.cloned.1.call-start = ((), (), s32[]{:S(2)}) async-start(), calls=%async_computation.5 | async-start | bytes 835584
  263.0 99.3 %copy-start.2 = (s32[512]{0:T(512)S(1)}, s32[512]{0:T(512)}, u32[]{:S(2)}) copy-start(s32[512]{0:T(512)} %param.8) | copy-start | bytes 6148
Sparse Core Ops, SparseCore 0:
  28.0 105.1 all-gather.3
  223.9 70.1 reduce-scatter.4
  298.5 239.1 reduce-scatter.6
